TPU v7x, 512 devices: a whole 4x4x16 slice. The times are simulated.
512 devices in a mesh: dp: 4 (over y), outer: 32 (over z, core), inner: 4 (over x).
Axes of the slice: x: 4, y: 4, z: 16, core: 2. Of those that a mesh axis runs over, the one named last changes fastest.
Arguments:
- query_rows: bfloat16 [65536, 256], P(('dp', 'outer', 'inner')), parts along dimension 0, may hold values from -8 to 8
- key_rows: bfloat16 [65536, 256], P(('dp', 'outer', 'inner')), parts along dimension 0, may hold values from -8 to 8
- value_rows: bfloat16 [65536, 1024], P(('dp', 'outer', 'inner')), parts along dimension 0, may hold values from -6 to 6
- conv_weight: float32 [3, 1024], replicated, may hold values from -1 to 1
- norm_gain: float32 [1024], replicated, may hold values from 0.1 to 1.9
Outputs:
- layer_out: bfloat16 [65536, 1024], P(('dp', 'outer', 'inner')), parts along dimension 0
There are 4 independent parts, one for each index of `dp`. A program takes and returns all parts, laid end to end along the dimension named above; an argument that names none is the same for every part. Nothing has to cross between parts.
All inputs are finite; a program needn't handle non-finite values.
Results may differ from a plain program's by a relative error of at most 0.013.
Values may be sent and summed in bfloat16 or wider, within the bound.
No kernel may reach another device: no remote copies, remote signals or barrier semaphores. Data moves between devices by JAX's collectives and lax.ppermute only.
A program may use at most 128 MiB of HBM per device.

v0:
```python
import math
import jax
import jax.numpy as jnp
from jax import lax
from jax.sharding import PartitionSpec as P

HEADS = 16
FEAT = 16
VDIM = 64
PHI = 273
TAPS = 3
WIN = 64
BLK = 128


def shifted(value, axis, steps):
    count = lax.axis_size(axis)
    initial, last = (max(0, -steps), min(count, count - steps))
    return lax.ppermute(value, axis, [(source, source + steps) for source in range(initial, last)])


def carried_in(shard, axis, combine, identity):
    count, position = (lax.axis_size(axis), lax.axis_index(axis))
    everything = lax.all_gather(shard.astype(jnp.bfloat16), axis)
    start = jnp.broadcast_to(jnp.asarray(identity, shard.dtype), shard.shape)

    def hop(k, before):
        reached = k < position
        new = combine(before, everything[k].astype(shard.dtype))
        return jnp.where(reached, new, before)

    return lax.fori_loop(0, count, hop, start)


def features(rows_in):
    entries = rows_in.astype(jnp.float32)
    leading = entries.shape[:-1]
    pair_terms = (entries[..., :, None] * entries[..., None, :]).reshape(leading + (FEAT * FEAT,))
    const_term = jnp.ones(leading + (1,), jnp.float32)
    joined = jnp.concatenate(
        [const_term, entries * (1.0 / FEAT**0.25), pair_terms * (1.0 / math.sqrt(2.0 * FEAT))],
        axis=-1,
    )
    return joined.astype(jnp.bfloat16)


def convolve(padded, conv_weight, out_rows):
    conv_sum = jnp.zeros((out_rows, padded.shape[1]), jnp.float32)
    for tap_index in range(TAPS):
        offset = TAPS - 1 - tap_index
        conv_sum = conv_sum + conv_weight[tap_index][None, :] * padded[
            offset : offset + out_rows
        ].astype(jnp.float32)
    return conv_sum.astype(jnp.bfloat16)


def add_states(earlier_part, later_part):
    return earlier_part + later_part


def on_device(query_rows, key_rows, value_rows, conv_weight, norm_gain):
    local_rows = query_rows.shape[0]
    lag_rows = TAPS - 1
    score_scale = 1.0 / math.sqrt(FEAT)
    block_index = lax.axis_index(("outer", "inner"))
    tail_conv = convolve(value_rows[local_rows - WIN - lag_rows :], conv_weight, WIN)
    prev_keys, prev_conv, prev_raw = shifted(
        (key_rows[local_rows - WIN :], tail_conv, value_rows[local_rows - lag_rows :]),
        ("outer", "inner"),
        1,
    )
    conv_rows = convolve(jnp.concatenate([prev_raw, value_rows], 0), conv_weight, local_rows)
    block_total = local_rows // BLK
    query_blocks = query_rows.reshape(block_total, BLK, HEADS, FEAT)
    key_blocks = key_rows.reshape(block_total, BLK, HEADS, FEAT)
    value_blocks = conv_rows.reshape(block_total, BLK, HEADS, VDIM)
    phi_key = features(key_blocks)
    block_states = jnp.einsum(
        "ntaf,ntac->nfac", phi_key, value_blocks, preferred_element_type=jnp.float32
    )
    local_before = jnp.concatenate(
        [jnp.zeros_like(block_states), jnp.cumsum(block_states[:-1], axis=0)], 0
    )
    local_total = local_before[-1] + block_states[-1]
    scores = (
        jnp.einsum("niaf,njaf->naij", query_blocks, key_blocks, preferred_element_type=jnp.float32)
        * score_scale
    )
    causal = jnp.arange(BLK)[:, None] >= jnp.arange(BLK)[None, :]
    intra_weights = jnp.where(causal[None, None], 1.0 + scores + 0.5 * scores * scores, 0.0).astype(
        jnp.bfloat16
    )
    own_part = jnp.einsum(
        "naij,njac->niac", intra_weights, value_blocks, preferred_element_type=jnp.float32
    )
    win_blocks = local_rows // WIN
    ext_keys = jnp.concatenate([prev_keys, key_rows], 0).reshape(win_blocks + 1, WIN, HEADS, FEAT)
    ext_conv = jnp.concatenate([prev_conv, conv_rows], 0).reshape(win_blocks + 1, WIN, HEADS, VDIM)
    near_keys = jnp.concatenate([ext_keys[:-1], ext_keys[1:]], axis=1)
    near_values = jnp.concatenate([ext_conv[:-1], ext_conv[1:]], axis=1)
    query_windows = query_rows.reshape(win_blocks, WIN, HEADS, FEAT)
    window_scores = (
        jnp.einsum("niaf,njaf->naij", query_windows, near_keys, preferred_element_type=jnp.float32)
        * score_scale
    )
    offset_rows = jnp.arange(2 * WIN)[None, :] - jnp.arange(WIN)[:, None]
    inside = (offset_rows >= 0) & (offset_rows <= WIN)
    position = (
        block_index * local_rows
        + jnp.arange(win_blocks, dtype=jnp.int32)[:, None] * WIN
        + jnp.arange(2 * WIN, dtype=jnp.int32)[None, :]
        - WIN
    )
    allowed = inside[None, None] & (position >= 0)[:, None, None, :]
    masked = jnp.where(allowed, window_scores, -1e30)
    row_max = jnp.max(masked, axis=-1, keepdims=True)
    exp_scores = jnp.where(allowed, jnp.exp(masked - row_max), 0.0)
    window_probs = (exp_scores / jnp.sum(exp_scores, axis=-1, keepdims=True)).astype(jnp.bfloat16)
    window_out = jnp.einsum(
        "naij,njac->niac", window_probs, near_values, preferred_element_type=jnp.float32
    )
    sent_state = local_total.reshape(PHI, HEADS * VDIM)
    zero_state = jnp.zeros(sent_state.shape, jnp.float32)
    group_sum = None
    inner_prefix = carried_in(sent_state, "inner", add_states, zero_state)
    group_sum = lax.psum(sent_state, "inner")
    outer_before = carried_in(group_sum, "outer", add_states, zero_state)
    carried = inner_prefix + outer_before
    carried = carried.reshape(PHI, HEADS, VDIM)
    state_rounded = (carried[None] + local_before).astype(jnp.bfloat16)
    phi_query = features(query_blocks)
    earlier_part = jnp.einsum(
        "ntaf,nfac->ntac", phi_query, state_rounded, preferred_element_type=jnp.float32
    )
    numerator = (own_part + earlier_part).reshape(local_rows, HEADS, VDIM)
    mean_square = jnp.mean(numerator * numerator, axis=-1, keepdims=True)
    linear_out = numerator * lax.rsqrt(mean_square + 1e-06) * norm_gain.reshape(HEADS, VDIM)
    mixed_heads = linear_out + window_out.reshape(local_rows, HEADS, VDIM)
    return mixed_heads.astype(jnp.bfloat16).reshape(local_rows, HEADS * VDIM)


def solution(mesh):
    in_specs = (
        P(("dp", "outer", "inner"), None),
        P(("dp", "outer", "inner"), None),
        P(("dp", "outer", "inner"), None),
        P(),
        P(),
    )
    out_specs = P(("dp", "outer", "inner"), None)
    return jax.shard_map(
        on_device, mesh=mesh, in_specs=in_specs, out_specs=out_specs, check_vma=False
    )
```

profile of v0, /device:TPU:1, one launch (start us, length us, event | category | flops | bytes accessed | tf_op | source)
XLA Modules:
  0.0 259.6 jit_solution(5805641317175301192)
XLA Ops:
  7.5 3.9 %collective-permute-start = (bf16[2,1024]{0,1:T(8,128)(2,1)S(1)}, bf16[2,1024]{0,1:T(8,128)(2,1)S(1)}, u32[]{:S(2)}, u32[]{:S(2)}) collective-permute-start(bf16[2,1024]{0,1:T(8,128)(2,1)S(1)} %copy.66), channel_id=1, source_target_pairs={{0,1},{1,2},{2,3},{3,4},{4,5},{5,6},{6,7},{7,8},{8,9},{9,10},{10,1... | collective-permute-start | bytes 12296 | tf_op jit(solution)/shard_map/ppermute | solution.py:19
  13.0 4.3 %collective-permute-done = bf16[2,1024]{0,1:T(8,128)(2,1)S(1)} collective-permute-done((bf16[2,1024]{0,1:T(8,128)(2,1)S(1)}, bf16[2,1024]{0,1:T(8,128)(2,1)S(1)}, u32[]{:S(2)}, u32[]{:S(2)}) %collective-permute-start) | collective-permute-done | bytes 4128 | tf_op jit(solution)/shard_map/ppermute | solution.py:19
  19.6 2.2 copy.70
  22.3 29.1 %all-reduce.1 = bf16[273,1024]{1,0:T(8,128)(2,1)} all-reduce(f32[273,1024]{1,0:T(8,128)S(1)} %copy.71), channel_id=1, replica_groups=mesh['dp'=4,'outer'=32,'inner'=4] {'inner'}, use_global_device_ids=true, to_apply=%region_2.3 | all-reduce | flops 279552 | bytes 1677312 | tf_op jit(solution)/shard_map/psum | solution.py:126
  52.8 2.1 collective-permute-start.1
  55.0 2.3 collective-permute-start.2
  63.2 10.6 %collective-permute-done.2 = bf16[64,256]{1,0:T(8,128)(2,1)S(1)} collective-permute-done((bf16[64,256]{1,0:T(8,128)(2,1)S(1)}, bf16[64,256]{1,0:T(8,128)(2,1)S(1)}, u32[]{:S(2)}, u32[]{:S(2)}) %collective-permute-start.2) | collective-permute-done | bytes 32800 | tf_op jit(solution)/shard_map/ppermute | solution.py:19
  74.1 1.9 fusion.77
  77.5 6.4 %convolution_bitcast_fusion = f32[2,64,16,64]{1,3,2,0:T(8,128)} fusion(bf16[2,64,16,64]{1,3,2,0:T(8,128)(2,1)} %copy.79, bf16[2,64,16,64]{1,3,2,0:T(8,128)(2,1)S(1)} %copy.78, f32[2,16,64]{2,1,0:T(8,128)S(1)} %fusion.77, pred[2,64,128]{2,1,0:T(8,128)(4,1)S(1)} %broadcast_and_fusion, bf16[2,64,16,16]{1,3,2,0:T(8,128)(2,1)} %copy.83, ...), kind=kOutput, calls=%fused_computation.9 | convolution fusion | flops 44828800 | bytes 1269760 | tf_op jit(solution)/shard_map/naij,njac->niac/dot_general | solution.py:119
  83.9 2.0 copy.93
  87.3 6.8 %while.28 = (s32[]{:T(128)}, f32[273,1024]{1,0:T(8,128)S(1)}, s32[]{:T(128)}, bf16[4,273,1024]{2,1,0:T(8,128)(2,1)}, s32[]{:T(128)}, /*index=5*/s32[]{:T(128)}) while((s32[]{:T(128)}, f32[273,1024]{1,0:T(8,128)S(1)}, s32[]{:T(128)}, bf16[4,273,1024]{2,1,0:T(8,128)(2,1)}, s32[]{:T(128)}, /*index=5*/s32[]{:T(128)}) %tuple.63), condition=%wide.region_1.2_spmd.clone, body=%wide.region_0.1_spmd.clone.sunk | while | flops 1118212 | bytes 2795613 | solution.py:32
  90.7 1.7 add_select_fusion.4
  92.4 1.7 add_select_fusion.4
  94.1 100.6 %all-gather.7.cloned.1.call-done = bf16[32,273,1024]{2,1,0:T(8,128)(2,1)} async-done(((bf16[1,273,1024]{2,1,0:T(8,128)(2,1)}), bf16[32,273,1024]{2,1,0:T(8,128)(2,1)}) %all-gather.7.cloned.1.call-update) | async-done | bytes 17891344 | tf_op jit(solution)/shard_map/all_gather | solution.py:24
  194.8 54.4 %while.29 = (s32[]{:T(128)}, f32[273,1024]{1,0:T(8,128)S(1)}, s32[]{:T(128)}, bf16[32,273,1024]{2,1,0:T(8,128)(2,1)}, s32[]{:T(128)}, /*index=5*/s32[]{:T(128)}) while((s32[]{:T(128)}, f32[273,1024]{1,0:T(8,128)S(1)}, s32[]{:T(128)}, bf16[32,273,1024]{2,1,0:T(8,128)(2,1)}, s32[]{:T(128)}, /*index=5*/s32[]{:T(128)}) %tuple.66), condition=%wide.region_4.5_spmd.clone, body=%wide.region_3.4_spmd.clone.sunk | while | flops 1118212 | bytes 2795613 | solution.py:32
  205.0 1.7 add_select_fusion.5
  206.7 1.7 add_select_fusion.5
  208.4 1.7 add_select_fusion.5
  210.1 1.7 add_select_fusion.5
  211.8 1.7 add_select_fusion.5
  213.5 1.7 add_select_fusion.5
  215.2 1.7 add_select_fusion.5
  237.3 1.7 add_select_fusion.5
  239.0 1.7 add_select_fusion.5
  (98 shorter events, 61.0 us)
Async XLA Ops:
  6.5 6.3 %copy-start.3 = (bf16[128,1024]{1,0:T(8,128)(2,1)S(1)}, bf16[128,1024]{1,0:T(8,128)(2,1)}, u32[]{:S(2)}) copy-start(bf16[128,1024]{1,0:T(8,128)(2,1)} %param.11) | copy-start | bytes 786436
  6.5 6.3 %copy-start.8 = (f32[3,1024]{1,0:T(4,128)S(1)}, f32[3,1024]{1,0:T(4,128)}, u32[]{:S(2)}) copy-start(f32[3,1024]{1,0:T(4,128)} %param.12) | copy-start | bytes 36868
  6.5 80.8 %all-gather.5.cloned.1.call-start = ((), (), s32[]{:S(2)}) async-start(), calls=%async_computation | async-start | bytes 2867200 | tf_op jit(solution)/shard_map/all_gather | solution.py:24
  7.5 9.8 %collective-permute-start = (bf16[2,1024]{0,1:T(8,128)(2,1)S(1)}, bf16[2,1024]{0,1:T(8,128)(2,1)S(1)}, u32[]{:S(2)}, u32[]{:S(2)}) collective-permute-start(bf16[2,1024]{0,1:T(8,128)(2,1)S(1)} %copy.66), channel_id=1, source_target_pairs={{0,1},{1,2},{2,3},{3,4},{4,5},{5,6},{6,7},{7,8},{8,9},{9,10},{10,1... | collective-permute-start | bytes 12296 | tf_op jit(solution)/shard_map/ppermute | solution.py:19
  21.9 172.9 %all-gather.7.cloned.1.call-start = ((), (), s32[]{:S(2)}) async-start(), calls=%async_computation.1 | async-start | bytes 18923520 | tf_op jit(solution)/shard_map/all_gather | solution.py:24
  51.4 3.6 %copy-start.2 = (bf16[128,256]{1,0:T(8,128)(2,1)S(1)}, bf16[128,256]{1,0:T(8,128)(2,1)}, u32[]{:S(2)}) copy-start(bf16[128,256]{1,0:T(8,128)(2,1)} %param.10) | copy-start | bytes 196612
  51.4 6.0 %copy-start.6 = (bf16[128,256]{1,0:T(8,128)(2,1)S(1)}, bf16[128,256]{1,0:T(8,128)(2,1)}, u32[]{:S(2)}) copy-start(bf16[128,256]{1,0:T(8,128)(2,1)} %param.9) | copy-start | bytes 196612
  52.8 23.2 %collective-permute-start.1 = (bf16[64,1024]{0,1:T(8,128)(2,1)}, bf16[64,1024]{0,1:T(8,128)(2,1)}, u32[]{:S(2)}, u32[]{:S(2)}) collective-permute-start(bf16[64,1024]{0,1:T(8,128)(2,1)} %add_convert_fusion.1), channel_id=1, source_target_pairs={{0,1},{1,2},{2,3},{3,4},{4,5},{5,6},{6,7},{7,8},{8,9},{9,10},{10,1... | collective-permute-start | bytes 393224 | tf_op jit(solution)/shard_map/ppermute | solution.py:19
  55.0 18.8 %collective-permute-start.2 = (bf16[64,256]{1,0:T(8,128)(2,1)S(1)}, bf16[64,256]{1,0:T(8,128)(2,1)S(1)}, u32[]{:S(2)}, u32[]{:S(2)}) collective-permute-start(bf16[64,256]{1,0:T(8,128)(2,1)S(1)} %slice.69), channel_id=1, source_target_pairs={{0,1},{1,2},{2,3},{3,4},{4,5},{5,6},{6,7},{7,8},{8,9},{9,10},{10,1... | collective-permute-start | bytes 98312 | tf_op jit(solution)/shard_map/ppermute | solution.py:19
  57.7 16.4 %copy-start.4 = (bf16[2,64,16,16]{1,0,3,2:T(2,128)(2,1)}, bf16[2,64,16,16]{1,0,3,2:T(2,128)(2,1)S(1)}, u32[]{:S(2)}) copy-start(bf16[2,64,16,16]{1,0,3,2:T(2,128)(2,1)S(1)} %reshape.244) | copy-start | bytes 196612
  74.1 1.9 copy-start.5
  249.2 1.0 copy-start.10
  249.4 1.3 copy-start.1
  249.4 1.3 copy-start.7
  250.7 1.0 copy-start
  250.7 1.0 copy-start.9
Sparse Core Ops, SparseCore 0:
  22.0 51.1 all-gather.4
  75.2 119.4 all-gather.6
where the time goes:
time: 262 us; the launch traced here: 260 us
  waiting for transfers between devices  116 us (44%)
  other arithmetic  66.4 us (25%)
  blocking collectives  29.1 us (11%)
  between operations  13.8 us (5%)
  local copies, waits for them, and re-layouts  13.5 us (5%)
  matrix products  12 us (5%)
  starting transfers between devices  8.44 us (3%)
    all_gather x2, waiting for transfers between devices, carried_in(): everything = lax.all_gather(shard.astype(jnp.bfloat16), axis)  101 us
    select_n x36, other arithmetic, hop(): return jnp.where(reached, new, before)  60.4 us
    psum x1, blocking collectives, on_device(): group_sum = lax.psum(sent_state, 'inner')  29.1 us
    ppermute x3, waiting for transfers between devices, shifted(): lax.ppermute(value, axis, [(source, source + steps) for source in range(i...  15 us
    ppermute x3, starting transfers between devices, shifted(): lax.ppermute(value, axis, [(source, source + steps) for source in range(i...  8.4 us
    dot_general x1, matrix products, on_device(): jnp.einsum('naij,njac->niac', window_probs, near_values, preferred_elemen...  6.4 us
  transfers between devices with their start and end apart: 5, of which 3 were waited for; matrix products, arithmetic and copies ran while one was open for 11% of the time, Pallas kernels for 0%

commit v1 on v0

--- a/solution.py
+++ b/solution.py
@@ -123,7 +123,7 @@
     zero_state = jnp.zeros(sent_state.shape, jnp.float32)
     group_sum = None
     inner_prefix = carried_in(sent_state, "inner", add_states, zero_state)
-    group_sum = lax.psum(sent_state, "inner")
+    group_sum = jnp.sum(lax.all_gather(sent_state, "inner"), axis=0)
     outer_before = carried_in(group_sum, "outer", add_states, zero_state)
     carried = inner_prefix + outer_before
     carried = carried.reshape(PHI, HEADS, VDIM)

time: 262 us -> 312 us (1.19)
  waiting for transfers between devices: 116 us -> 189 us
  blocking collectives: 29.1 us -> 0 us
    all_gather x0 -> x1, waiting for transfers between devices: none -> 62.5 us  [on_device(): group_sum = jnp.sum(lax.all_gather(sent_state, 'inner'), axis=0)]
    psum x1 -> x0, blocking collectives: 29.1 us -> none  [on_device(): group_sum = lax.psum(sent_state, 'inner')]
    all_gather x2, waiting for transfers between devices: 101 us -> 122 us  [carried_in(): everything = lax.all_gather(shard.astype(jnp.bfloat16), axis)]
    ppermute x3, waiting for transfers between devices: 15 us -> 4.33 us  [shifted(): lax.ppermute(value, axis, [(source, source + steps) for source in range(i...]
  transfers between devices with their start and end apart: 5 -> 6, of which waited for: 3 -> 4; matrix products, arithmetic and copies ran while one was open for 11% -> 11% of each run, Pallas kernels for 0% -> 0%
where the time goes in v1:
time: 312 us; the launch traced here: 310 us
  waiting for transfers between devices  189 us (61%)
  other arithmetic  69.5 us (22%)
  local copies, waits for them, and re-layouts  15.7 us (5%)
  between operations  13.5 us (4%)
  matrix products  11.8 us (4%)
  starting transfers between devices  9.55 us (3%)
    all_gather x2, waiting for transfers between devices, carried_in(): everything = lax.all_gather(shard.astype(jnp.bfloat16), axis)  122 us
    all_gather x1, waiting for transfers between devices, on_device(): group_sum = jnp.sum(lax.all_gather(sent_state, 'inner'), axis=0)  62.5 us
    select_n x36, other arithmetic, hop(): return jnp.where(reached, new, before)  60.4 us
    ppermute x3, starting transfers between devices, shifted(): lax.ppermute(value, axis, [(source, source + steps) for source in range(i...  9.47 us
    dot_general x1, matrix products, on_device(): jnp.einsum('naij,njac->niac', window_probs, near_values, preferred_elemen...  6.38 us
  transfers between devices with their start and end apart: 6, of which 4 were waited for; matrix products, arithmetic and copies ran while one was open for 11% of the time, Pallas kernels for 0%

profile of v1, /device:TPU:1, one launch (start us, length us, event | category | flops | bytes accessed | tf_op | source)
XLA Modules:
  0.0 309.8 jit_solution(4261989005177549827)
XLA Ops:
  7.5 3.9 %collective-permute-start = (bf16[2,1024]{0,1:T(8,128)(2,1)S(1)}, bf16[2,1024]{0,1:T(8,128)(2,1)S(1)}, u32[]{:S(2)}, u32[]{:S(2)}) collective-permute-start(bf16[2,1024]{0,1:T(8,128)(2,1)S(1)} %copy.66), channel_id=1, source_target_pairs={{0,1},{1,2},{2,3},{3,4},{4,5},{5,6},{6,7},{7,8},{8,9},{9,10},{10,1... | collective-permute-start | bytes 12296 | tf_op jit(solution)/shard_map/ppermute | solution.py:19
  13.0 4.3 %collective-permute-done = bf16[2,1024]{0,1:T(8,128)(2,1)S(1)} collective-permute-done((bf16[2,1024]{0,1:T(8,128)(2,1)S(1)}, bf16[2,1024]{0,1:T(8,128)(2,1)S(1)}, u32[]{:S(2)}, u32[]{:S(2)}) %collective-permute-start) | collective-permute-done | bytes 4128 | tf_op jit(solution)/shard_map/ppermute | solution.py:19
  22.5 62.5 %all-gather.8.cloned.1.call-done = f32[4,273,1024]{2,1,0:T(8,128)} async-done(((f32[1,273,1024]{2,1,0:T(8,128)}), f32[4,273,1024]{2,1,0:T(8,128)}) %all-gather.8.cloned.1.call-update) | async-done | bytes 4472848 | tf_op jit(solution)/shard_map/all_gather | solution.py:126
  85.0 2.8 reduce_sum.27
  90.1 2.5 collective-permute-start.1
  92.6 3.0 collective-permute-start.2
  102.3 2.6 fusion.77
  106.5 6.4 %convolution_bitcast_fusion = f32[2,64,16,64]{1,3,2,0:T(8,128)} fusion(bf16[2,64,16,64]{1,3,2,0:T(8,128)(2,1)} %copy.81, bf16[2,64,16,64]{1,3,2,0:T(8,128)(2,1)S(1)} %copy.80, f32[2,16,64]{2,1,0:T(8,128)} %fusion.77, pred[2,64,128]{2,1,0:T(8,128)(4,1)S(1)} %broadcast_and_fusion, bf16[2,64,16,16]{1,3,2,0:T(8,128)(2,1)} %copy.85, ...), kind=kOutput, calls=%fused_computation.8 | convolution fusion | flops 44828800 | bytes 1269760 | tf_op jit(solution)/shard_map/naij,njac->niac/dot_general | solution.py:119
  112.8 2.1 copy.95
  116.3 11.5 %all-gather.6.cloned.1.call-done = bf16[4,273,1024]{2,1,0:T(8,128)(2,1)} async-done(((bf16[1,273,1024]{2,1,0:T(8,128)(2,1)}), bf16[4,273,1024]{2,1,0:T(8,128)(2,1)}) %all-gather.6.cloned.1.call-update) | async-done | bytes 2236432 | tf_op jit(solution)/shard_map/all_gather | solution.py:24
  127.8 6.8 %while.28 = (s32[]{:T(128)}, f32[273,1024]{1,0:T(8,128)S(1)}, s32[]{:T(128)}, bf16[4,273,1024]{2,1,0:T(8,128)(2,1)}, s32[]{:T(128)}, /*index=5*/s32[]{:T(128)}) while((s32[]{:T(128)}, f32[273,1024]{1,0:T(8,128)S(1)}, s32[]{:T(128)}, bf16[4,273,1024]{2,1,0:T(8,128)(2,1)}, s32[]{:T(128)}, /*index=5*/s32[]{:T(128)}) %tuple.62), condition=%wide.region_1.2_spmd.clone, body=%wide.region_0.1_spmd.clone.sunk | while | flops 1118212 | bytes 2795613 | solution.py:32
  129.5 1.7 add_select_fusion.4
  131.2 1.7 add_select_fusion.4
  132.9 1.7 add_select_fusion.4
  134.6 110.6 %all-gather.10.cloned.1.call-done = bf16[32,273,1024]{2,1,0:T(8,128)(2,1)} async-done(((bf16[1,273,1024]{2,1,0:T(8,128)(2,1)}), bf16[32,273,1024]{2,1,0:T(8,128)(2,1)}) %all-gather.10.cloned.1.call-update) | async-done | bytes 17891344 | tf_op jit(solution)/shard_map/all_gather | solution.py:24
  245.2 54.4 %while.29 = (s32[]{:T(128)}, f32[273,1024]{1,0:T(8,128)S(1)}, s32[]{:T(128)}, bf16[32,273,1024]{2,1,0:T(8,128)(2,1)}, s32[]{:T(128)}, /*index=5*/s32[]{:T(128)}) while((s32[]{:T(128)}, f32[273,1024]{1,0:T(8,128)S(1)}, s32[]{:T(128)}, bf16[32,273,1024]{2,1,0:T(8,128)(2,1)}, s32[]{:T(128)}, /*index=5*/s32[]{:T(128)}) %tuple.65), condition=%wide.region_4.5_spmd.clone, body=%wide.region_3.4_spmd.clone.sunk | while | flops 1118212 | bytes 2795613 | solution.py:32
  246.9 1.7 add_select_fusion.5
  269.0 1.7 add_select_fusion.5
  270.7 1.7 add_select_fusion.5
  272.4 1.7 add_select_fusion.5
  274.1 1.7 add_select_fusion.5
  275.8 1.7 add_select_fusion.5
  277.5 1.7 add_select_fusion.5
  279.2 1.7 add_select_fusion.5
  (109 shorter events, 64.7 us)
Async XLA Ops:
  6.5 6.3 %copy-start.4 = (bf16[128,1024]{1,0:T(8,128)(2,1)S(1)}, bf16[128,1024]{1,0:T(8,128)(2,1)}, u32[]{:S(2)}) copy-start(bf16[128,1024]{1,0:T(8,128)(2,1)} %param.11) | copy-start | bytes 786436
  6.5 6.3 %copy-start.9 = (f32[3,1024]{1,0:T(4,128)S(1)}, f32[3,1024]{1,0:T(4,128)}, u32[]{:S(2)}) copy-start(f32[3,1024]{1,0:T(4,128)} %param.12) | copy-start | bytes 36868
  6.5 78.5 %all-gather.8.cloned.1.call-start = ((), (), s32[]{:S(2)}) async-start(), calls=%async_computation.1 | async-start | bytes 5734400 | tf_op jit(solution)/shard_map/all_gather | solution.py:126
  7.5 9.8 %collective-permute-start = (bf16[2,1024]{0,1:T(8,128)(2,1)S(1)}, bf16[2,1024]{0,1:T(8,128)(2,1)S(1)}, u32[]{:S(2)}, u32[]{:S(2)}) collective-permute-start(bf16[2,1024]{0,1:T(8,128)(2,1)S(1)} %copy.66), channel_id=1, source_target_pairs={{0,1},{1,2},{2,3},{3,4},{4,5},{5,6},{6,7},{7,8},{8,9},{9,10},{10,1... | collective-permute-start | bytes 12296 | tf_op jit(solution)/shard_map/ppermute | solution.py:19
  13.0 5.7 %copy-start.11 = (bf16[273]{0:T(512)(128)(2,1)}, bf16[273]{0:T(512)(128)(2,1)S(1)}, u32[]{:S(2)}) copy-start(bf16[273]{0:T(512)(128)(2,1)S(1)} %pad.11.clone) | copy-start | bytes 1642
  20.2 1.3 copy-start
  20.3 107.5 %all-gather.6.cloned.1.call-start = ((), (), s32[]{:S(2)}) async-start(), calls=%async_computation | async-start | bytes 2867200 | tf_op jit(solution)/shard_map/all_gather | solution.py:24
  22.4 222.7 %all-gather.10.cloned.1.call-start = ((), (), s32[]{:S(2)}) async-start(), calls=%async_computation.2 | async-start | bytes 18923520 | tf_op jit(solution)/shard_map/all_gather | solution.py:24
  89.4 3.3 %copy-start.3 = (bf16[128,256]{1,0:T(8,128)(2,1)S(1)}, bf16[128,256]{1,0:T(8,128)(2,1)}, u32[]{:S(2)}) copy-start(bf16[128,256]{1,0:T(8,128)(2,1)} %param.10) | copy-start | bytes 196612
  89.4 6.4 %copy-start.7 = (bf16[128,256]{1,0:T(8,128)(2,1)S(1)}, bf16[128,256]{1,0:T(8,128)(2,1)}, u32[]{:S(2)}) copy-start(bf16[128,256]{1,0:T(8,128)(2,1)} %param.9) | copy-start | bytes 196612
  90.1 14.9 %collective-permute-start.1 = (bf16[64,1024]{0,1:T(8,128)(2,1)S(1)}, bf16[64,1024]{0,1:T(8,128)(2,1)}, u32[]{:S(2)}, u32[]{:S(2)}) collective-permute-start(bf16[64,1024]{0,1:T(8,128)(2,1)S(1)} %add_convert_fusion.1), channel_id=1, source_target_pairs={{0,1},{1,2},{2,3},{3,4},{4,5},{5,6},{6,7},{7,8},{8,9},{9,10},{10,1... | collective-permute-start | bytes 393224 | tf_op jit(solution)/shard_map/ppermute | solution.py:19
  92.6 9.4 %collective-permute-start.2 = (bf16[64,256]{1,0:T(8,128)(2,1)S(1)}, bf16[64,256]{1,0:T(8,128)(2,1)S(1)}, u32[]{:S(2)}, u32[]{:S(2)}) collective-permute-start(bf16[64,256]{1,0:T(8,128)(2,1)S(1)} %slice.69), channel_id=1, source_target_pairs={{0,1},{1,2},{2,3},{3,4},{4,5},{5,6},{6,7},{7,8},{8,9},{9,10},{10,1... | collective-permute-start | bytes 98312 | tf_op jit(solution)/shard_map/ppermute | solution.py:19
  102.3 2.6 copy-start.6
  104.9 1.5 copy-start.5
  299.6 1.0 copy-start.13
  299.8 1.3 copy-start.2
  299.9 1.3 copy-start.8
  299.9 1.2 copy-start.12
  301.1 1.0 copy-start.1
  301.1 1.0 copy-start.10
Sparse Core Ops, SparseCore 0:
  20.4 64.5 all-gather.7
  87.1 40.5 all-gather.5
  129.9 115.2 all-gather.9
